TPU v7x, 32 devices: a whole 2x2x4 slice. The times are simulated.
32 devices in a mesh: dp: 8 (over z, x), tensor: 4 (over y, core).
Axes of the slice: x: 2, y: 2, z: 4, core: 2. Of those that a mesh axis runs over, the one named last changes fastest.
Arguments:
- tokens: bfloat16 [16384, 1024], P(('dp', 'tensor')), may hold values from -6 to 6
- cotangent: bfloat16 [16384, 1024], P(('dp', 'tensor')), may hold values from -6 to 6
- lengths: int32 [8, 16], P('dp'), may hold values from 1 to 256, 2048 in all within a row
- qkv_master: float32 [1024, 3, 1024], P('dp', None, 'tensor'), may hold values from -0.1875 to 0.1875
- qkv_first: float32 [1024, 3, 1024], P('dp', None, 'tensor'), may hold values from -0.00015258789 to 0.00015258789
- qkv_second: float32 [1024, 3, 1024], P('dp', None, 'tensor'), may hold values from 2.9798684e-11 to 4.7677895e-10
- out_master: float32 [1024, 1024], P(('tensor', 'dp')), may hold values from -1 to 1
- out_first: float32 [1024, 1024], P(('tensor', 'dp')), may hold values from -9.1552734e-05 to 9.1552734e-05
- out_second: float32 [1024, 1024], P(('tensor', 'dp')), may hold values from 5.959737e-12 to 9.535579e-11
- in_master: float32 [1024, 2, 4096], P('dp', None, 'tensor'), may hold values from -0.1875 to 0.1875
- in_first: float32 [1024, 2, 4096], P('dp', None, 'tensor'), may hold values from -0.00015258789 to 0.00015258789
- in_second: float32 [1024, 2, 4096], P('dp', None, 'tensor'), may hold values from 2.9798684e-11 to 4.7677895e-10
- down_master: float32 [4096, 1024], P(('tensor', 'dp')), may hold values from -0.09375 to 0.09375
- down_first: float32 [4096, 1024], P(('tensor', 'dp')), may hold values from -0.00015258789 to 0.00015258789
- down_second: float32 [4096, 1024], P(('tensor', 'dp')), may hold values from 2.9798684e-11 to 4.7677895e-10
- norm_gains: float32 [2, 1024], replicated, may hold values from 0.2 to 2.8
- gain_first: float32 [2, 1024], replicated, may hold values from -0.00061035156 to 0.00061035156
- gain_second: float32 [2, 1024], replicated, may hold values from 4.7677895e-10 to 7.628463e-09
Outputs:
- layer_out: bfloat16 [16384, 1024], P(('dp', 'tensor'))
- input_grad: float32 [16384, 1024], P(('dp', 'tensor'))
- qkv_grad: float32 [1024, 3, 1024], P('dp', None, 'tensor')
- qkv_new: float32 [1024, 3, 1024], P('dp', None, 'tensor')
- qkv_first_new: float32 [1024, 3, 1024], P('dp', None, 'tensor')
- qkv_second_new: float32 [1024, 3, 1024], P('dp', None, 'tensor')
- out_grad: float32 [1024, 1024], P(('tensor', 'dp'))
- out_new: float32 [1024, 1024], P(('tensor', 'dp'))
- out_first_new: float32 [1024, 1024], P(('tensor', 'dp'))
- out_second_new: float32 [1024, 1024], P(('tensor', 'dp'))
- in_grad: float32 [1024, 2, 4096], P('dp', None, 'tensor')
- in_new: float32 [1024, 2, 4096], P('dp', None, 'tensor')
- in_first_new: float32 [1024, 2, 4096], P('dp', None, 'tensor')
- in_second_new: float32 [1024, 2, 4096], P('dp', None, 'tensor')
- down_grad: float32 [4096, 1024], P(('tensor', 'dp'))
- down_new: float32 [4096, 1024], P(('tensor', 'dp'))
- down_first_new: float32 [4096, 1024], P(('tensor', 'dp'))
- down_second_new: float32 [4096, 1024], P(('tensor', 'dp'))
- gain_grad: float32 [2, 1024], replicated
- gain_new: float32 [2, 1024], replicated
- gain_first_new: float32 [2, 1024], replicated
- gain_second_new: float32 [2, 1024], replicated
- grad_norm: float32 [], replicated
Inputs may be any that keep to these rules, and one draw needn't show every extreme that they name: Each row's 16 window lengths are positive, add up to 2048, and the longest is 256.
All inputs are finite; a program needn't handle non-finite values.
Results may differ from a plain program's by a relative error of at most 0.024.
Values may be sent and summed in bfloat16 or wider, within the bound.
No kernel may reach another device: no remote copies, remote signals or barrier semaphores. Data moves between devices by JAX's collectives and lax.ppermute only.
A program may use at most 192 MiB of HBM per device.

v0:
```python
from functools import partial
import math
import jax
import jax.numpy as jnp
from jax import lax
from jax.sharding import PartitionSpec as P

D = 1024
HEADS = 16
HEAD_DIM = 64
FF = 4096
ROW = 2048
STEP = 5
eps_norm = 1e-05
beta_one = 0.9
beta_two = 0.999
learn_rate = 0.05
gain_rate = 0.6
weight_decay = 0.1
adam_eps = 1e-08
max_norm = 1.0


def layer_norm(values, gain):
    centre = values - jnp.mean(values, axis=-1, keepdims=True)
    spread = jnp.mean(centre * centre, axis=-1, keepdims=True)
    return centre * lax.rsqrt(spread + eps_norm) * gain


def row_layout(lengths):
    seg_ends = jnp.cumsum(lengths, axis=-1)
    places = jnp.arange(ROW, dtype=jnp.int32)
    passed = (places[:, None] >= seg_ends[..., None, :]).astype(jnp.int32)
    segment = jnp.sum(passed, axis=-1)
    offset = places - jnp.sum(passed * lengths[..., None, :], axis=-1)
    return (segment, offset)


def rotary_tables(offset):
    half_dim = HEAD_DIM // 2
    inverse = jnp.exp(
        jnp.arange(half_dim, dtype=jnp.float32) * (-2.0 * math.log(10000.0) / HEAD_DIM)
    )
    angles = offset.astype(jnp.float32)[..., None] * inverse
    return (jnp.cos(angles), jnp.sin(angles))


def rotate(values, cosine, sine):
    half_dim = values.shape[-1] // 2
    front_half = values[..., :half_dim]
    back_half = values[..., half_dim:]
    cos_wide = cosine[..., None, :]
    sin_wide = sine[..., None, :]
    return jnp.concatenate(
        [
            front_half * cos_wide - back_half * sin_wide,
            back_half * cos_wide + front_half * sin_wide,
        ],
        axis=-1,
    )


def swiglu(gate_up):
    half_cols = gate_up.shape[-1] // 2
    return jax.nn.silu(gate_up[:, :half_cols]) * gate_up[:, half_cols:]


def adam_update(weight, first_moment, second_moment, gradient, factor, use_decay, rate):
    clipped = gradient * factor
    first_new = beta_one * first_moment + (1.0 - beta_one) * clipped
    second_new = beta_two * second_moment + (1.0 - beta_two) * clipped * clipped
    first_hat = first_new / (1.0 - beta_one**STEP)
    second_hat = second_new / (1.0 - beta_two**STEP)
    direction = first_hat / (jnp.sqrt(second_hat) + adam_eps) + use_decay * weight_decay * weight
    return (clipped, weight - rate * direction, first_new, second_new)


def contract_rows(left, right):
    return lax.dot_general(
        left, right, (((0,), (0,)), ((), ())), preferred_element_type=jnp.float32
    )


def contract_cols(left, right):
    return lax.dot_general(
        left, right, (((1,), (1,)), ((), ())), preferred_element_type=jnp.float32
    )


def per_device(
    tokens,
    cotangent,
    lengths,
    qkv_master,
    qkv_first,
    qkv_second,
    out_master,
    out_first,
    out_second,
    in_master,
    in_first,
    in_second,
    down_master,
    down_first,
    down_second,
    norm_gains,
    gain_first,
    gain_second,
):
    heads_local = HEADS // lax.axis_size("tensor")
    width_local = heads_local * HEAD_DIM
    ffn_local = FF // lax.axis_size("tensor")
    row_count = lengths.shape[0]
    all_rows = row_count * ROW
    score_scale = HEAD_DIM ** (-0.5)
    block_rows = min(512, ROW)
    block_count = ROW // block_rows
    w_qkv, w_out, w_in, w_down = (
        lax.all_gather(qkv_master.astype(jnp.bfloat16), "dp", axis=0, tiled=True),
        lax.all_gather(out_master.astype(jnp.bfloat16), "dp", axis=0, tiled=True),
        lax.all_gather(in_master.astype(jnp.bfloat16), "dp", axis=0, tiled=True),
        lax.all_gather(down_master.astype(jnp.bfloat16), "dp", axis=0, tiled=True),
    )
    w_qkv = w_qkv.reshape(D, 3 * width_local)
    w_in = w_in.reshape(D, 2 * ffn_local)
    segment, offset = row_layout(lengths)
    cosine, sine = rotary_tables(offset)
    gain_one = norm_gains[0]
    gain_two = norm_gains[1]
    inputs = tokens.astype(jnp.float32)
    normed = layer_norm(inputs, gain_one)
    gathered_one = lax.all_gather(normed.astype(jnp.bfloat16), "tensor", axis=0, tiled=True)
    projected = jnp.dot(gathered_one, w_qkv, preferred_element_type=jnp.float32)
    projected = projected.reshape(row_count, ROW, 3, heads_local, HEAD_DIM)
    queries = rotate(projected[:, :, 0], cosine, sine).astype(jnp.bfloat16)
    keys = rotate(projected[:, :, 1], cosine, sine).astype(jnp.bfloat16)
    values = projected[:, :, 2].astype(jnp.bfloat16)

    def score_block(query_block, key_row, segment_block, segment_row):
        scores = (
            jnp.einsum("qhd,khd->hqk", query_block, key_row, preferred_element_type=jnp.float32)
            * score_scale
        )
        allowed = segment_block[:, None] == segment_row[None, :]
        return jnp.where(allowed[None], scores, -1e30)

    def forward_row(pieces):
        query_row, key_row, value_row, segment_row = pieces

        def forward_block(block_parts):
            query_block, segment_block = block_parts
            masked = score_block(query_block, key_row, segment_block, segment_row)
            row_max = jnp.max(masked, axis=-1, keepdims=True)
            log_total = (
                jnp.log(jnp.sum(jnp.exp(masked - row_max), axis=-1, keepdims=True)) + row_max
            )
            weights = jnp.exp(masked - log_total).astype(jnp.bfloat16)
            mixed_heads = jnp.einsum(
                "hqk,khd->qhd", weights, value_row, preferred_element_type=jnp.float32
            )
            return (mixed_heads.astype(jnp.bfloat16), log_total)

        return lax.map(
            forward_block,
            (
                query_row.reshape(block_count, block_rows, heads_local, HEAD_DIM),
                segment_row.reshape(block_count, block_rows),
            ),
        )

    mixed_heads, log_totals = lax.map(forward_row, (queries, keys, values, segment))
    attended = mixed_heads.reshape(all_rows, width_local)
    middle = inputs + lax.psum_scatter(
        jnp.dot(attended, w_out, preferred_element_type=jnp.float32),
        "tensor",
        scatter_dimension=0,
        tiled=True,
    )
    normed_two = layer_norm(middle, gain_two)
    gathered_two = lax.all_gather(normed_two.astype(jnp.bfloat16), "tensor", axis=0, tiled=True)
    gate_up = jnp.dot(gathered_two, w_in, preferred_element_type=jnp.float32)
    hidden = swiglu(gate_up).astype(jnp.bfloat16)
    output = middle + lax.psum_scatter(
        jnp.dot(hidden, w_down, preferred_element_type=jnp.float32).astype(jnp.bfloat16),
        "tensor",
        scatter_dimension=0,
        tiled=True,
    ).astype(jnp.float32)
    layer_out = output.astype(jnp.bfloat16)
    upstream = cotangent.astype(jnp.float32)
    gathered_down = lax.all_gather(cotangent, "tensor", axis=0, tiled=True)
    grad_down = contract_rows(hidden, gathered_down)
    hidden_grad = contract_cols(gathered_down, w_down)
    gate_up_grad = jax.vjp(swiglu, gate_up)[1](hidden_grad)[0].astype(jnp.bfloat16)
    grad_in = contract_rows(gathered_two, gate_up_grad)
    normed_two_grad = lax.psum_scatter(
        contract_cols(gate_up_grad, w_in).astype(jnp.bfloat16),
        "tensor",
        scatter_dimension=0,
        tiled=True,
    ).astype(jnp.float32)
    middle_back, gain_two_grad = jax.vjp(layer_norm, middle, gain_two)[1](normed_two_grad)
    middle_grad = upstream + middle_back
    gathered_mid = lax.all_gather(middle_grad.astype(jnp.bfloat16), "tensor", axis=0, tiled=True)
    grad_out = contract_rows(attended, gathered_mid)
    attended_grad = contract_cols(gathered_mid, w_out).astype(jnp.bfloat16)
    attended_grad = attended_grad.reshape(row_count, ROW, heads_local, HEAD_DIM)

    def backward_row(pieces):
        query_row, key_row, value_row, segment_row, total_row, grad_row = pieces

        def backward_block(running, block_parts):
            key_acc, value_acc = running
            query_block, segment_block, total_block, grad_block = block_parts
            masked = score_block(query_block, key_row, segment_block, segment_row)
            probs_block = jnp.exp(masked - total_block)
            probs_low = probs_block.astype(jnp.bfloat16)
            prob_grad = jnp.einsum(
                "qhd,khd->hqk", grad_block, value_row, preferred_element_type=jnp.float32
            )
            row_inner = jnp.sum(probs_block * prob_grad, axis=-1, keepdims=True)
            score_grad = (probs_block * (prob_grad - row_inner)).astype(jnp.bfloat16)
            query_grad = (
                jnp.einsum("hqk,khd->qhd", score_grad, key_row, preferred_element_type=jnp.float32)
                * score_scale
            )
            key_acc = (
                key_acc
                + jnp.einsum(
                    "hqk,qhd->khd", score_grad, query_block, preferred_element_type=jnp.float32
                )
                * score_scale
            )
            value_acc = value_acc + jnp.einsum(
                "hqk,qhd->khd", probs_low, grad_block, preferred_element_type=jnp.float32
            )
            return ((key_acc, value_acc), query_grad)

        zeros_acc = jnp.zeros((ROW, heads_local, HEAD_DIM), jnp.float32)
        block_inputs = (
            query_row.reshape(block_count, block_rows, heads_local, HEAD_DIM),
            segment_row.reshape(block_count, block_rows),
            total_row,
            grad_row.reshape(block_count, block_rows, heads_local, HEAD_DIM),
        )
        (key_grad, value_grad), query_grad = lax.scan(
            backward_block, (zeros_acc, zeros_acc), block_inputs
        )
        return (query_grad.reshape(ROW, heads_local, HEAD_DIM), key_grad, value_grad)

    query_grad, key_grad, value_grad = lax.map(
        backward_row, (queries, keys, values, segment, log_totals, attended_grad)
    )
    rotate_back = jax.vjp(partial(rotate, cosine=cosine, sine=sine), projected[:, :, 0])[1]
    query_raw = rotate_back(query_grad)[0]
    key_raw = rotate_back(key_grad)[0]
    qkv_grad_low = (
        jnp.stack([query_raw, key_raw, value_grad], axis=2)
        .reshape(all_rows, 3 * width_local)
        .astype(jnp.bfloat16)
    )
    grad_qkv = contract_rows(gathered_one, qkv_grad_low)
    normed_grad = lax.psum_scatter(
        contract_cols(qkv_grad_low, w_qkv).astype(jnp.bfloat16),
        "tensor",
        scatter_dimension=0,
        tiled=True,
    ).astype(jnp.float32)
    input_back, gain_one_grad = jax.vjp(layer_norm, inputs, gain_one)[1](normed_grad)
    input_grad = middle_grad + input_back
    reduced_qkv, reduced_out, reduced_in, reduced_down = (
        lax.psum_scatter(
            grad_qkv.reshape(D, 3, width_local).astype(jnp.bfloat16),
            "dp",
            scatter_dimension=0,
            tiled=True,
        ).astype(jnp.float32),
        lax.psum_scatter(
            grad_out.astype(jnp.bfloat16), "dp", scatter_dimension=0, tiled=True
        ).astype(jnp.float32),
        lax.psum_scatter(
            grad_in.reshape(D, 2, ffn_local).astype(jnp.bfloat16),
            "dp",
            scatter_dimension=0,
            tiled=True,
        ).astype(jnp.float32),
        lax.psum_scatter(
            grad_down.astype(jnp.bfloat16), "dp", scatter_dimension=0, tiled=True
        ).astype(jnp.float32),
    )
    local_squares = (
        jnp.sum(reduced_qkv * reduced_qkv)
        + jnp.sum(reduced_out * reduced_out)
        + jnp.sum(reduced_in * reduced_in)
        + jnp.sum(reduced_down * reduced_down)
    )
    gain_part = jnp.stack([gain_one_grad, gain_two_grad])
    gain_total, weight_squares = lax.psum((gain_part, local_squares), ("dp", "tensor"))
    grad_norm = jnp.sqrt(weight_squares + jnp.sum(gain_total * gain_total))
    factor = max_norm / jnp.maximum(grad_norm, max_norm)
    qkv_res = adam_update(qkv_master, qkv_first, qkv_second, reduced_qkv, factor, 1.0, learn_rate)
    out_res = adam_update(out_master, out_first, out_second, reduced_out, factor, 1.0, learn_rate)
    in_res = adam_update(in_master, in_first, in_second, reduced_in, factor, 1.0, learn_rate)
    down_res = adam_update(
        down_master, down_first, down_second, reduced_down, factor, 1.0, learn_rate
    )
    gain_res = adam_update(norm_gains, gain_first, gain_second, gain_total, factor, 0.0, gain_rate)
    return (
        layer_out,
        input_grad,
        qkv_res[0],
        qkv_res[1],
        qkv_res[2],
        qkv_res[3],
        out_res[0],
        out_res[1],
        out_res[2],
        out_res[3],
        in_res[0],
        in_res[1],
        in_res[2],
        in_res[3],
        down_res[0],
        down_res[1],
        down_res[2],
        down_res[3],
        gain_res[0],
        gain_res[1],
        gain_res[2],
        gain_res[3],
        grad_norm,
    )


def solution(mesh):
    placed = (
        P(("dp", "tensor"), None),
        P(("dp", "tensor"), None),
        P("dp", None),
        P("dp", None, "tensor"),
        P("dp", None, "tensor"),
        P("dp", None, "tensor"),
        P(("tensor", "dp"), None),
        P(("tensor", "dp"), None),
        P(("tensor", "dp"), None),
        P("dp", None, "tensor"),
        P("dp", None, "tensor"),
        P("dp", None, "tensor"),
        P(("tensor", "dp"), None),
        P(("tensor", "dp"), None),
        P(("tensor", "dp"), None),
        P(),
        P(),
        P(),
    )
    return jax.shard_map(
        per_device,
        mesh=mesh,
        in_specs=placed,
        out_specs=(
            P(("dp", "tensor"), None),
            P(("dp", "tensor"), None),
            P("dp", None, "tensor"),
            P("dp", None, "tensor"),
            P("dp", None, "tensor"),
            P("dp", None, "tensor"),
            P(("tensor", "dp"), None),
            P(("tensor", "dp"), None),
            P(("tensor", "dp"), None),
            P(("tensor", "dp"), None),
            P("dp", None, "tensor"),
            P("dp", None, "tensor"),
            P("dp", None, "tensor"),
            P("dp", None, "tensor"),
            P(("tensor", "dp"), None),
            P(("tensor", "dp"), None),
            P(("tensor", "dp"), None),
            P(("tensor", "dp"), None),
            P(),
            P(),
            P(),
            P(),
            P(),
        ),
        check_vma=False,
    )
```

profile of v0, /device:TPU:0, one launch (start us, length us, event | category | flops | bytes accessed | tf_op | source)
XLA Modules:
  0.0 1104.4 jit_solution(1875028781626215786)
XLA Ops:
  16.8 36.3 %all_gather.26 = bf16[256,1024]{1,0:T(8,128)(2,1)} all-gather(bf16[32,1024]{1,0:T(8,128)(2,1)S(1)} %convert_element_type.159), channel_id=1, replica_groups=mesh['dp'=8,'tensor'=4] {'dp'}, dimensions={0}, use_global_device_ids=true | all-gather | bytes 589824 | tf_op jit(solution)/shard_map/all_gather | solution.py:120
  54.1 7.5 all-gather.10.cloned.1.call-done
  61.6 35.9 %all-gather.8.cloned.1.call-done = bf16[2048,1024]{1,0:T(8,128)(2,1)} async-done(((bf16[512,1024]{1,0:T(8,128)(2,1)}), bf16[2048,1024]{1,0:T(8,128)(2,1)}) %all-gather.8.cloned.1.call-update) | async-done | bytes 4194320 | tf_op jit(solution)/shard_map/all_gather | solution.py:132
  97.5 6.2 fusion.48
  110.1 57.2 %while.47 = (s32[]{:T(128)}, bf16[4,512,4,64]{1,3,2,0:T(8,128)(2,1)}, f32[4,4,512,1]{2,1,3,0:T(4,128)}, s32[4,512]{1,0:T(4,128)S(1)}, s32[2048]{0:T(1024)S(1)}, ...) while((s32[]{:T(128)}, ...), condition=%wide.region_8.9_spmd, body=%wide.region_5.8_spmd.sunk | while | flops 1121056768 | bytes 57227380 | solution.py:163
  119.0 5.5 fusion.144
  178.4 69.5 %reduce-scatter.8.cloned.1.call-done = f32[512,1024]{1,0:T(8,128)} async-done(((f32[2048,1024]{1,0:T(8,128)}), f32[512,1024]{1,0:T(8,128)}) %reduce-scatter.8.cloned.1.call-update) | async-done | bytes 2097168 | tf_op jit(solution)/shard_map/reduce_scatter | solution.py:173
  254.4 69.7 %all-gather.14.cloned.1.call-done = bf16[1024,2,1024]{2,1,0:T(2,128)(2,1)} async-done(((bf16[128,2,1024]{2,1,0:T(2,128)(2,1)}), bf16[1024,2,1024]{2,1,0:T(2,128)(2,1)}) %all-gather.14.cloned.1.call-update) | async-done | bytes 4194320 | tf_op jit(solution)/shard_map/all_gather | solution.py:121
  324.1 5.6 copy.103
  329.7 29.2 %all-gather.12.cloned.1.call-done = bf16[2048,1024]{1,0:T(8,128)(2,1)} async-done(((bf16[512,1024]{1,0:T(8,128)(2,1)}), bf16[2048,1024]{1,0:T(8,128)(2,1)}) %all-gather.12.cloned.1.call-update) | async-done | bytes 4194320 | tf_op jit(solution)/shard_map/all_gather | solution.py:180
  358.9 15.1 %fusion.96 = f32[2048,2048]{1,0:T(8,128)} fusion(bf16[2048,1024]{1,0:T(8,128)(2,1)} %all-gather.12.cloned.1.call-done, bf16[1024,2048]{1,0:T(8,128)(2,1)} %bitcast.176), kind=kOutput, calls=%fused_computation.180 | convolution fusion | flops 8589934592 | bytes 25165824 | tf_op jit(solution)/shard_map/dot_general | solution.py:181
  374.0 37.0 %all-gather.16.cloned.1.call-done = bf16[1024,1024]{1,0:T(8,128)(2,1)} async-done(((bf16[128,1024]{1,0:T(8,128)(2,1)}), bf16[1024,1024]{1,0:T(8,128)(2,1)}) %all-gather.16.cloned.1.call-update) | async-done | bytes 2097168 | tf_op jit(solution)/shard_map/all_gather | solution.py:122
  411.0 34.6 %all-gather.18.cloned.1.call-done = bf16[2048,1024]{1,0:T(8,128)(2,1)} async-done(((bf16[512,1024]{1,0:T(8,128)(2,1)}), bf16[2048,1024]{1,0:T(8,128)(2,1)}) %all-gather.18.cloned.1.call-update) | async-done | bytes 4194320 | tf_op jit(solution)/shard_map/all_gather | solution.py:191
  445.6 17.2 %fusion.73 = (f32[2048,1024]{1,0:T(8,128)}, f32[2048,1024]{1,0:T(8,128)}, bf16[2048,1024]{1,0:T(8,128)(2,1)}) fusion(f32[2048,2048]{1,0:T(8,128)} %fusion.96, bf16[2048,1024]{1,0:T(8,128)(2,1)} %all-gather.18.cloned.1.call-done, bf16[1024,1024]{1,0:T(8,128)(2,1)} %all-gather.16.cloned.1.call-done), kind=kOutput, calls=%fused_computation.124 | convolution fusion | flops 4324327424 | bytes 44040192 | tf_op jit(solution)/shard_map/dot_general | solution.py:85
  462.8 15.0 %convolution_convert_fusion.1 = bf16[2048,1024]{1,0:T(8,128)(2,1)} fusion(bf16[1024,2048]{1,0:T(8,128)(2,1)} %bitcast.177, f32[2048,1024]{1,0:T(8,128)} %get-tuple-element.338, f32[2048,1024]{1,0:T(8,128)} %get-tuple-element.337), kind=kOutput, calls=%fused_computation.65 | convolution fusion | flops 8600420352 | bytes 25165824 | tf_op jit(solution)/shard_map/dot_general | solution.py:85
  478.4 9.6 convolution_convert_fusion.3
  488.0 34.6 %reduce-scatter.12.cloned.1.call-done = bf16[512,1024]{1,0:T(8,128)(2,1)} async-done(((bf16[2048,1024]{1,0:T(8,128)(2,1)}), bf16[512,1024]{1,0:T(8,128)(2,1)}) %reduce-scatter.12.cloned.1.call-update) | async-done | bytes 1048592 | tf_op jit(solution)/shard_map/reduce_scatter | solution.py:196
  525.3 44.4 %reduce-scatter.10.cloned.1.call-done = bf16[512,1024]{1,0:T(8,128)(2,1)} async-done(((bf16[2048,1024]{1,0:T(8,128)(2,1)}), bf16[512,1024]{1,0:T(8,128)(2,1)}) %reduce-scatter.10.cloned.1.call-update) | async-done | bytes 1048592 | tf_op jit(solution)/shard_map/reduce_scatter | solution.py:183
  575.8 17.0 %convolution_convert_fusion = bf16[1024,2048]{1,0:T(8,128)(2,1)} fusion(bf16[2048,1024]{1,0:T(8,128)(2,1)} %all-gather.12.cloned.1.call-done, f32[2048,1024]{1,0:T(8,128)} %get-tuple-element.338, f32[2048,1024]{1,0:T(8,128)} %get-tuple-element.337), kind=kOutput, calls=%fused_computation.64 | convolution fusion | flops 8600420352 | bytes 25165824 | tf_op jit(solution)/shard_map/dot_general | solution.py:79
  592.8 7.9 convert_element_type.182
  600.8 9.4 convolution_convert_fusion.5
  620.5 230.1 %while.48 = (s32[]{:T(128)}, f32[2048,4,64]{0,2,1:T(8,128)}, f32[2048,4,64]{0,2,1:T(8,128)}, f32[4,512,4,64]{1,0,3,2:T(4,128)}, bf16[4,512,4,64]{1,3,2,0:T(8,128...) while((s32[]{:T(128)}, f32[2048,4,64]{0,2,1:T(8,128)}, ...), condition=%wide.region_18.19_spmd.clone, body=%wide.region_16.18_spmd.clone.sunk | while | flops 2751068160 | bytes 183179600 | solution.py:246
  625.6 7.2 fusion.156
  632.8 11.5 %multiply_reduce_fusion.4 = (f32[4,512]{1,0:T(4,128)}, f32[4,512,2048]{2,1,0:T(8,128)}) fusion(f32[4,512,2048]{2,1,0:T(8,128)S(1)} %fusion.154, f32[4,512]{1,0:T(4,128)S(1)} %dynamic-slice_bitcast_fusion.2, pred[512,2048]{1,0:T(8,128)(4,1)} %copy-done.1, bf16[2048,4,64]{0,2,1:T(8,128)(2,1)} %get-tuple-element.552, ...), kind=kOutput, calls=%fused_computation.20.clone.1 | convolution fusion | flops 557840384 | bytes 35930116 | tf_op jit(solution)/shard_map/while/body/eval_jaxpr/while/body/eval_jaxpr/qhd,khd->hqk/dot_general | solution.py:218
  644.4 11.2 %multiply_convert_fusion.4 = bf16[4,512,2048]{2,1,0:T(8,128)(2,1)} fusion(f32[4,512,2048]{2,1,0:T(8,128)} %get-tuple-element.487, f32[4,512,2048]{2,1,0:T(8,128)S(1)} %fusion.154, f32[4,512]{1,0:T(4,128)} %get-tuple-element.488, f32[4,512]{1,0:T(4,128)S(1)} %dynamic-slice_bitcast_fusion.2, pred[512,2048]{1,0:T(8,128)(4,1)} %copy-done.1), kind=kLoop, calls=%fused_computation.19.clone.1 | loop fusion | flops 25165824 | bytes 43008000 | tf_op jit(solution)/shard_map/while/body/eval_jaxpr/while/body/eval_jaxpr/convert_element_type | solution.py:222
  655.5 6.2 fusion.157
  666.2 11.1 %dynamic_update_slice.33 = f32[4,512,4,64]{1,0,3,2:T(4,128)} dynamic-update-slice(f32[4,512,4,64]{1,0,3,2:T(4,128)} %get-tuple-element.532, f32[1,512,4,64]{1,0,3,2:T(1,128)S(1)} %copy.107, s32[]{:T(128)S(6)} %copy.125, s32[]{:T(128)} %constant.79.clone.1..sunk, s32[]{:T(128)} %constant.79.clone.1..sunk, s32[]{:T(128)} %constant.79.clone.1..sunk) | dynamic-update-slice | bytes 1048580 | tf_op jit(solution)/shard_map/while/body/eval_jaxpr/while/body/jit(dynamic_update_index_in_dim)/dynamic_update_slice | solution.py:246
  682.2 7.6 fusion.156
  689.9 11.5 %multiply_reduce_fusion.4 = (f32[4,512]{1,0:T(4,128)}, f32[4,512,2048]{2,1,0:T(8,128)}) fusion(f32[4,512,2048]{2,1,0:T(8,128)S(1)} %fusion.154, f32[4,512]{1,0:T(4,128)S(1)} %dynamic-slice_bitcast_fusion.2, pred[512,2048]{1,0:T(8,128)(4,1)} %copy-done.1, bf16[2048,4,64]{0,2,1:T(8,128)(2,1)} %get-tuple-element.552, ...), kind=kOutput, calls=%fused_computation.20.clone.1 | convolution fusion | flops 557840384 | bytes 35930116 | tf_op jit(solution)/shard_map/while/body/eval_jaxpr/while/body/eval_jaxpr/qhd,khd->hqk/dot_general | solution.py:218
  701.4 11.0 %multiply_convert_fusion.4 = bf16[4,512,2048]{2,1,0:T(8,128)(2,1)} fusion(f32[4,512,2048]{2,1,0:T(8,128)} %get-tuple-element.487, f32[4,512,2048]{2,1,0:T(8,128)S(1)} %fusion.154, f32[4,512]{1,0:T(4,128)} %get-tuple-element.488, f32[4,512]{1,0:T(4,128)S(1)} %dynamic-slice_bitcast_fusion.2, pred[512,2048]{1,0:T(8,128)(4,1)} %copy-done.1), kind=kLoop, calls=%fused_computation.19.clone.1 | loop fusion | flops 25165824 | bytes 43008000 | tf_op jit(solution)/shard_map/while/body/eval_jaxpr/while/body/eval_jaxpr/convert_element_type | solution.py:222
  712.5 6.2 fusion.157
  723.9 11.1 %dynamic_update_slice.33 = f32[4,512,4,64]{1,0,3,2:T(4,128)} dynamic-update-slice(f32[4,512,4,64]{1,0,3,2:T(4,128)} %get-tuple-element.532, f32[1,512,4,64]{1,0,3,2:T(1,128)S(1)} %copy.107, s32[]{:T(128)S(6)} %copy.125, s32[]{:T(128)} %constant.79.clone.1..sunk, s32[]{:T(128)} %constant.79.clone.1..sunk, s32[]{:T(128)} %constant.79.clone.1..sunk) | dynamic-update-slice | bytes 1048580 | tf_op jit(solution)/shard_map/while/body/eval_jaxpr/while/body/jit(dynamic_update_index_in_dim)/dynamic_update_slice | solution.py:246
  740.0 7.6 fusion.156
  747.6 11.5 %multiply_reduce_fusion.4 = (f32[4,512]{1,0:T(4,128)}, f32[4,512,2048]{2,1,0:T(8,128)}) fusion(f32[4,512,2048]{2,1,0:T(8,128)S(1)} %fusion.154, f32[4,512]{1,0:T(4,128)S(1)} %dynamic-slice_bitcast_fusion.2, pred[512,2048]{1,0:T(8,128)(4,1)} %copy-done.1, bf16[2048,4,64]{0,2,1:T(8,128)(2,1)} %get-tuple-element.552, ...), kind=kOutput, calls=%fused_computation.20.clone.1 | convolution fusion | flops 557840384 | bytes 35930116 | tf_op jit(solution)/shard_map/while/body/eval_jaxpr/while/body/eval_jaxpr/qhd,khd->hqk/dot_general | solution.py:218
  759.2 11.0 multiply_convert_fusion.4
  770.2 6.2 fusion.157
  781.6 11.1 %dynamic_update_slice.33 = f32[4,512,4,64]{1,0,3,2:T(4,128)} dynamic-update-slice(f32[4,512,4,64]{1,0,3,2:T(4,128)} %get-tuple-element.532, f32[1,512,4,64]{1,0,3,2:T(1,128)S(1)} %copy.107, s32[]{:T(128)S(6)} %copy.125, s32[]{:T(128)} %constant.79.clone.1..sunk, s32[]{:T(128)} %constant.79.clone.1..sunk, s32[]{:T(128)} %constant.79.clone.1..sunk) | dynamic-update-slice | bytes 1048580 | tf_op jit(solution)/shard_map/while/body/eval_jaxpr/while/body/jit(dynamic_update_index_in_dim)/dynamic_update_slice | solution.py:246
  797.6 7.6 fusion.156
  805.3 11.5 %multiply_reduce_fusion.4 = (f32[4,512]{1,0:T(4,128)}, f32[4,512,2048]{2,1,0:T(8,128)}) fusion(f32[4,512,2048]{2,1,0:T(8,128)S(1)} %fusion.154, f32[4,512]{1,0:T(4,128)S(1)} %dynamic-slice_bitcast_fusion.2, pred[512,2048]{1,0:T(8,128)(4,1)} %copy-done.1, bf16[2048,4,64]{0,2,1:T(8,128)(2,1)} %get-tuple-element.552, ...), kind=kOutput, calls=%fused_computation.20.clone.1 | convolution fusion | flops 557840384 | bytes 35930116 | tf_op jit(solution)/shard_map/while/body/eval_jaxpr/while/body/eval_jaxpr/qhd,khd->hqk/dot_general | solution.py:218
  816.8 11.0 multiply_convert_fusion.4
  827.9 6.2 fusion.157
  839.3 11.1 %dynamic_update_slice.33 = f32[4,512,4,64]{1,0,3,2:T(4,128)} dynamic-update-slice(f32[4,512,4,64]{1,0,3,2:T(4,128)} %get-tuple-element.532, f32[1,512,4,64]{1,0,3,2:T(1,128)S(1)} %copy.107, s32[]{:T(128)S(6)} %copy.125, s32[]{:T(128)} %constant.79.clone.1..sunk, s32[]{:T(128)} %constant.79.clone.1..sunk, s32[]{:T(128)} %constant.79.clone.1..sunk) | dynamic-update-slice | bytes 1048580 | tf_op jit(solution)/shard_map/while/body/eval_jaxpr/while/body/jit(dynamic_update_index_in_dim)/dynamic_update_slice | solution.py:246
  870.1 7.0 convolution_convert_fusion.2
  883.5 37.6 %reduce-scatter.18.cloned.1.call-done = bf16[32,1024]{1,0:T(8,128)(2,1)} async-done(((bf16[256,1024]{1,0:T(8,128)(2,1)}), bf16[32,1024]{1,0:T(8,128)(2,1)}) %reduce-scatter.18.cloned.1.call-update) | async-done | bytes 65552 | tf_op jit(solution)/shard_map/reduce_scatter | solution.py:278
  922.6 66.9 %reduce-scatter.16.cloned.1.call-done = bf16[128,3,256]{2,0,1:T(8,128)(2,1)} async-done(((bf16[1024,3,256]{2,0,1:T(8,128)(2,1)}), bf16[128,3,256]{2,0,1:T(8,128)(2,1)}) %reduce-scatter.16.cloned.1.call-update) | async-done | bytes 196624 | tf_op jit(solution)/shard_map/reduce_scatter | solution.py:272
  993.7 41.8 %reduce-scatter.14.cloned.1.call-done = bf16[512,1024]{1,0:T(8,128)(2,1)} async-done(((bf16[2048,1024]{1,0:T(8,128)(2,1)}), bf16[512,1024]{1,0:T(8,128)(2,1)}) %reduce-scatter.14.cloned.1.call-update) | async-done | bytes 1048592 | tf_op jit(solution)/shard_map/reduce_scatter | solution.py:263
  1039.7 39.7 %all-reduce.7 = (f32[]{:T(128)}, f32[2,1024]{1,0:T(2,128)S(1)}) all-reduce(f32[]{:T(128)S(6)} %add.210, f32[2,1024]{1,0:T(2,128)S(1)} %pad_maximum_fusion.1), channel_id=1, replica_groups=mesh['dp'=8,'tensor'=4] {'dp','tensor'}, use_global_device_ids=true, to_apply=%region_30.31 | all-reduce | flops 2049 | bytes 16392 | tf_op jit(solution)/shard_map/psum | solution.py:298
  1086.4 6.5 multiply_subtract_fusion
  (297 shorter events, 186.4 us)
Async XLA Ops:
  7.2 9.1 copy-start.52
  7.2 9.6 copy-start.29
  7.2 54.4 %all-gather.10.cloned.1.call-start = ((), (), s32[]{:S(2)}) async-start(), calls=%async_computation.8 | async-start | bytes 1769472 | tf_op jit(solution)/shard_map/all_gather | solution.py:119
  9.1 88.4 %all-gather.8.cloned.1.call-start = ((), (), s32[]{:S(2)}) async-start(), calls=%async_computation.7 | async-start | bytes 5242880 | tf_op jit(solution)/shard_map/all_gather | solution.py:132
  16.3 231.6 %reduce-scatter.8.cloned.1.call-start = ((), (), s32[]{:S(2)}) async-start(), calls=%async_computation.9 | async-start | bytes 10485760 | tf_op jit(solution)/shard_map/reduce_scatter | solution.py:173
  54.1 50.3 %copy-start.14 = (f32[2048,32]{0,1:T(8,128)}, f32[2048,32]{0,1:T(8,128)S(1)}, u32[]{:S(2)}) copy-start(f32[2048,32]{0,1:T(8,128)S(1)} %get-tuple-element.355) | copy-start | bytes 786436
  54.1 50.3 %copy-start.16 = (f32[2048,32]{0,1:T(8,128)}, f32[2048,32]{0,1:T(8,128)S(1)}, u32[]{:S(2)}) copy-start(f32[2048,32]{0,1:T(8,128)S(1)} %get-tuple-element.356) | copy-start | bytes 786436
  167.3 8.6 copy-start.4
  167.3 8.6 copy-start.5
  176.0 148.1 %all-gather.14.cloned.1.call-start = ((), (), s32[]{:S(2)}) async-start(), calls=%async_computation.11 | async-start | bytes 4718592 | tf_op jit(solution)/shard_map/all_gather | solution.py:121
  178.4 180.5 %all-gather.12.cloned.1.call-start = ((), (), s32[]{:S(2)}) async-start(), calls=%async_computation.10 | async-start | bytes 5242880 | tf_op jit(solution)/shard_map/all_gather | solution.py:180
  251.7 159.3 %all-gather.16.cloned.1.call-start = ((), (), s32[]{:S(2)}) async-start(), calls=%async_computation.12 | async-start | bytes 2359296 | tf_op jit(solution)/shard_map/all_gather | solution.py:122
  253.6 192.1 %all-gather.18.cloned.1.call-start = ((), (), s32[]{:S(2)}) async-start(), calls=%async_computation.14 | async-start | bytes 5242880 | tf_op jit(solution)/shard_map/all_gather | solution.py:191
  254.3 268.3 %reduce-scatter.12.cloned.1.call-start = ((), (), s32[]{:S(2)}) async-start(), calls=%async_computation.15 | async-start | bytes 5242880 | tf_op jit(solution)/shard_map/reduce_scatter | solution.py:196
  477.9 91.8 %reduce-scatter.10.cloned.1.call-start = ((), (), s32[]{:S(2)}) async-start(), calls=%async_computation.13 | async-start | bytes 5242880 | tf_op jit(solution)/shard_map/reduce_scatter | solution.py:183
  488.0 122.4 %all-gather.20.cloned.1.call-start = ((), (), s32[]{:S(2)}) async-start(), calls=%async_computation.16 | async-start | bytes 5242880 | tf_op jit(solution)/shard_map/all_gather | solution.py:204
  573.1 19.7 %copy-start.45 = (f32[512]{0:T(512)}, f32[512]{0:T(512)S(1)}, u32[]{:S(2)}) copy-start(f32[512]{0:T(512)S(1)} %negate_multiply_fusion.1) | copy-start | bytes 6148
  575.7 303.3 %all-reduce.10.cloned.1.call-start = ((), (), s32[]{:S(2)}) async-start(), calls=%async_computation.21 | async-start | bytes 8388608
  600.7 281.1 %reduce-scatter.20.cloned.1.call-start = ((), (), s32[]{:S(2)}) async-start(), calls=%async_computation.20 | async-start | bytes 2359296 | tf_op jit(solution)/shard_map/reduce_scatter | solution.py:287
  600.8 9.6 copy-start.19
  610.3 310.8 %reduce-scatter.18.cloned.1.call-start = ((), (), s32[]{:S(2)}) async-start(), calls=%async_computation.19 | async-start | bytes 589824 | tf_op jit(solution)/shard_map/reduce_scatter | solution.py:278
  661.7 15.6 %copy-start.22 = (s32[2048]{0:T(1024)S(1)}, s32[2048]{0:T(1024)}, u32[]{:S(2)}) copy-start(s32[2048]{0:T(1024)} %copy-done.21) | copy-start | bytes 24580 | tf_op jit(solution)/shard_map/while/body/eval_jaxpr/while
  661.7 15.6 %copy-start.39 = (s32[4,512]{1,0:T(4,128)S(1)}, s32[4,512]{1,0:T(4,128)}, u32[]{:S(2)}) copy-start(s32[4,512]{1,0:T(4,128)} %copy-done.38) | copy-start | bytes 24580 | tf_op jit(solution)/shard_map/while/body/eval_jaxpr/while
  718.7 16.4 %copy-start.22 = (s32[2048]{0:T(1024)S(1)}, s32[2048]{0:T(1024)}, u32[]{:S(2)}) copy-start(s32[2048]{0:T(1024)} %copy-done.21) | copy-start | bytes 24580 | tf_op jit(solution)/shard_map/while/body/eval_jaxpr/while
  718.7 16.4 %copy-start.39 = (s32[4,512]{1,0:T(4,128)S(1)}, s32[4,512]{1,0:T(4,128)}, u32[]{:S(2)}) copy-start(s32[4,512]{1,0:T(4,128)} %copy-done.38) | copy-start | bytes 24580 | tf_op jit(solution)/shard_map/while/body/eval_jaxpr/while
  776.4 16.3 %copy-start.22 = (s32[2048]{0:T(1024)S(1)}, s32[2048]{0:T(1024)}, u32[]{:S(2)}) copy-start(s32[2048]{0:T(1024)} %copy-done.21) | copy-start | bytes 24580 | tf_op jit(solution)/shard_map/while/body/eval_jaxpr/while
  776.4 16.3 %copy-start.39 = (s32[4,512]{1,0:T(4,128)S(1)}, s32[4,512]{1,0:T(4,128)}, u32[]{:S(2)}) copy-start(s32[4,512]{1,0:T(4,128)} %copy-done.38) | copy-start | bytes 24580 | tf_op jit(solution)/shard_map/while/body/eval_jaxpr/while
  834.1 16.3 %copy-start.22 = (s32[2048]{0:T(1024)S(1)}, s32[2048]{0:T(1024)}, u32[]{:S(2)}) copy-start(s32[2048]{0:T(1024)} %copy-done.21) | copy-start | bytes 24580 | tf_op jit(solution)/shard_map/while/body/eval_jaxpr/while
  834.1 16.3 %copy-start.39 = (s32[4,512]{1,0:T(4,128)S(1)}, s32[4,512]{1,0:T(4,128)}, u32[]{:S(2)}) copy-start(s32[4,512]{1,0:T(4,128)} %copy-done.38) | copy-start | bytes 24580 | tf_op jit(solution)/shard_map/while/body/eval_jaxpr/while
  858.7 130.7 %reduce-scatter.16.cloned.1.call-start = ((), (), s32[]{:S(2)}) async-start(), calls=%async_computation.18 | async-start | bytes 1769472 | tf_op jit(solution)/shard_map/reduce_scatter | solution.py:272
  870.1 165.4 %reduce-scatter.14.cloned.1.call-start = ((), (), s32[]{:S(2)}) async-start(), calls=%async_computation.17 | async-start | bytes 5242880 | tf_op jit(solution)/shard_map/reduce_scatter | solution.py:263
  877.2 158.3 %copy-start.3 = (bf16[512,1024]{1,0:T(8,128)(2,1)S(1)}, bf16[512,1024]{1,0:T(8,128)(2,1)}, u32[]{:S(2)}) copy-start(bf16[512,1024]{1,0:T(8,128)(2,1)} %param.22) | copy-start | bytes 3145732
  877.2 158.3 %copy-start.37 = (f32[1,1024]{1,0:T(1,128)S(1)}, f32[1,1024]{1,0:T(1,128)}, u32[]{:S(2)}) copy-start(f32[1,1024]{1,0:T(1,128)} %copy-done.36) | copy-start | bytes 12292
  877.2 158.3 %copy-start.41 = (f32[512]{0:T(512)S(1)}, f32[512]{0:T(512)}, u32[]{:S(2)}) copy-start(f32[512]{0:T(512)} %copy-done.40) | copy-start | bytes 6148
  877.2 160.1 %copy-start.48 = (f32[512]{0:T(512)S(1)}, f32[512]{0:T(512)}, u32[]{:S(2)}) copy-start(f32[512]{0:T(512)} %copy-done.47) | copy-start | bytes 6148
  877.2 160.1 %copy-start.44 = (f32[512]{0:T(512)S(1)}, f32[512]{0:T(512)}, u32[]{:S(2)}) copy-start(f32[512]{0:T(512)} %copy-done.43) | copy-start | bytes 6148
  877.2 162.5 %copy-start.49 = (f32[1024]{0:T(1024)S(1)}, f32[1024]{0:T(1024)}, u32[]{:S(2)}) copy-start(f32[1024]{0:T(1024)} %get-tuple-element.261) | copy-start | bytes 12292
  877.2 204.3 %copy-start.42 = (f32[2,1024]{1,0:T(2,128)S(1)}, f32[2,1024]{1,0:T(2,128)}, u32[]{:S(2)}) copy-start(f32[2,1024]{1,0:T(2,128)} %param.37) | copy-start | bytes 24580
  877.2 204.3 %copy-start.50 = (f32[2,1024]{1,0:T(2,128)S(1)}, f32[2,1024]{1,0:T(2,128)}, u32[]{:S(2)}) copy-start(f32[2,1024]{1,0:T(2,128)} %param.38) | copy-start | bytes 24580
  877.2 204.3 %copy-start.51 = (f32[2,1024]{1,0:T(2,128)S(1)}, f32[2,1024]{1,0:T(2,128)}, u32[]{:S(2)}) copy-start(f32[2,1024]{1,0:T(2,128)} %param.39) | copy-start | bytes 24580
  877.3 204.9 %copy-start.7 = (f32[512,1024]{1,0:T(8,128)S(1)}, f32[512,1024]{1,0:T(8,128)}, u32[]{:S(2)}) copy-start(f32[512,1024]{1,0:T(8,128)} %copy-done.6) | copy-start | bytes 6291460
  877.3 204.9 %copy-start.46 = (f32[512]{0:T(512)S(1)}, f32[512]{0:T(512)}, u32[]{:S(2)}) copy-start(f32[512]{0:T(512)} %copy-done.45) | copy-start | bytes 6148
  1086.3 7.4 copy-start.20
  1086.3 7.4 copy-start.26
  1086.3 8.6 copy-start.17
  1086.3 8.6 copy-start.25
  1086.4 8.6 copy-start.27
  1086.4 8.6 copy-start.28
  (41 other events, 149.8 us)
Sparse Core Ops, SparseCore 0:
  10.7 50.9 all-gather.9
  63.8 33.7 all-gather.7
  176.1 71.7 reduce-scatter.7
  250.6 73.3 all-gather.13
  326.1 32.7 all-gather.11
  361.7 49.2 all-gather.15
  412.6 32.9 all-gather.17
  478.0 44.5 reduce-scatter.11
  525.1 44.5 reduce-scatter.9
  575.9 34.4 all-gather.19
  614.5 156.3 all-reduce.9
  774.7 66.9 reduce-scatter.19
  858.9 62.1 reduce-scatter.17
  925.0 64.4 reduce-scatter.15
  992.0 43.4 reduce-scatter.13
where the time goes:
time: 1110 us; the launch traced here: 1100 us
  waiting for transfers between devices  510 us (46%)
  matrix products  283 us (25%)
  other arithmetic  125 us (11%)
  local copies, waits for them, and re-layouts  88.5 us (8%)
  blocking collectives  76 us (7%)
  between operations  20.7 us (2%)
    all_gather x1, waiting for transfers between devices, per_device(): lax.all_gather(in_master.astype(jnp.bfloat16), 'dp', axis=0, tiled=True)  69.7 us
    reduce_scatter x1, waiting for transfers between devices, per_device(): lax.psum_scatter(jnp.dot(attended, w_out, preferred_element_type=jnp.floa...  69.5 us
    reduce_scatter x1, waiting for transfers between devices, per_device(): lax.psum_scatter(grad_qkv.reshape(D, 3, width_local).astype(jnp.bfloat16)...  66.9 us
    dynamic_update_slice x8, local copies, waits for them, and re-layouts, backward_row(): lax.scan(backward_block, (zeros_acc, zeros_acc), block_inputs)  46.6 us
    dot_general x4, matrix products, backward_block(): jnp.einsum('qhd,khd->hqk', grad_block, value_row, preferred_element_type=...  46.1 us
    reduce_scatter x1, waiting for transfers between devices, per_device(): lax.psum_scatter(jnp.dot(hidden, w_down, preferred_element_type=jnp.float...  44.4 us
    convert_element_type x4, other arithmetic, backward_block(): score_grad = (probs_block * (prob_grad - row_inner)).astype(jnp.bfloat16)  44.2 us
    dot_general x4, matrix products, contract_cols(): lax.dot_general(left, right, (((1,), (1,)), ((), ())), preferred_element_...  43.7 us
  transfers between devices with their start and end apart: 15, of which 13 were waited for; matrix products, arithmetic and copies ran while one was open for 32% of the time, Pallas kernels for 0%

commit v1 on v0

--- a/solution.py
+++ b/solution.py
@@ -19,6 +19,27 @@
 weight_decay = 0.1
 adam_eps = 1e-08
 max_norm = 1.0
+
+
+def gather_around(shard, axis, dim):
+    peers, index, span = (lax.axis_size(axis), lax.axis_index(axis), shard.shape[dim])
+    ahead = [(i, (i + 1) % peers) for i in range(peers)]
+    backward = [(i, (i - 1) % peers) for i in range(peers)]
+    out = jnp.zeros((*shard.shape[:dim], peers * span, *shard.shape[dim + 1 :]), shard.dtype)
+    out = lax.dynamic_update_slice_in_dim(out, shard, index * span, axis=dim)
+    from_left = from_right = shard
+    half = peers // 2
+    for step in range(1, half + 1):
+        from_left = lax.ppermute(from_left, axis, ahead)
+        out = lax.dynamic_update_slice_in_dim(
+            out, from_left, (index - step) % peers * span, axis=dim
+        )
+        if step < peers - half:
+            from_right = lax.ppermute(from_right, axis, backward)
+            out = lax.dynamic_update_slice_in_dim(
+                out, from_right, (index + step) % peers * span, axis=dim
+            )
+    return out
 
 
 def layer_norm(values, gain):
@@ -118,7 +139,7 @@
     w_qkv, w_out, w_in, w_down = (
         lax.all_gather(qkv_master.astype(jnp.bfloat16), "dp", axis=0, tiled=True),
         lax.all_gather(out_master.astype(jnp.bfloat16), "dp", axis=0, tiled=True),
-        lax.all_gather(in_master.astype(jnp.bfloat16), "dp", axis=0, tiled=True),
+        gather_around(in_master.astype(jnp.bfloat16), "dp", 0),
         lax.all_gather(down_master.astype(jnp.bfloat16), "dp", axis=0, tiled=True),
     )
     w_qkv = w_qkv.reshape(D, 3 * width_local)

time: 1110 us -> 1060 us (0.955)
  waiting for transfers between devices: 510 us -> 424 us
  starting transfers between devices: 1.2 us -> 19.5 us
  local copies, waits for them, and re-layouts: 88.5 us -> 105 us
    ppermute x0 -> x7, waiting for transfers between devices: none -> 74.5 us  [the longest x4 74.5 us: gather_around(): from_left = lax.ppermute(from_left, axis, ahead)]
    all_gather x1 -> x0, waiting for transfers between devices: 69.7 us -> none  [per_device(): lax.all_gather(in_master.astype(jnp.bfloat16), 'dp', axis=0, tiled=True)]
    all_gather x1, waiting for transfers between devices: 37 us -> 0.01 us  [per_device(): lax.all_gather(down_master.astype(jnp.bfloat16), 'dp', axis=0, tiled=True)]
    all_gather x1, waiting for transfers between devices: 29.2 us -> 0.01 us  [per_device(): lax.all_gather(normed_two.astype(jnp.bfloat16), 'tensor', axis=0, tiled=T...]
    all_gather x1, waiting for transfers between devices: 34.6 us -> 8.26 us  [per_device(): gathered_down = lax.all_gather(cotangent, 'tensor', axis=0, tiled=True)]
    ppermute x0 -> x7, starting transfers between devices: none -> 18.6 us  [the longest x3 9.59 us: gather_around(): from_right = lax.ppermute(from_right, axis, backward)]
    dynamic_update_slice x0 -> x7, local copies, waits for them, and re-layouts: none -> 13.3 us  [the longest x4 7.78 us: gather_around(): lax.dynamic_update_slice_in_dim(out, from_left, (index - step) % peers *...]
  transfers between devices with their start and end apart: 15 -> 21, of which waited for: 13 -> 13; matrix products, arithmetic and copies ran while one was open for 32% -> 35% of each run, Pallas kernels for 0% -> 0%
where the time goes in v1:
time: 1060 us
  waiting for transfers between devices  424 us (40%)
  matrix products  283 us (27%)
  other arithmetic  125 us (12%)
  local copies, waits for them, and re-layouts  105 us (10%)
  blocking collectives  76 us (7%)
  between operations  20.7 us (2%)
  starting transfers between devices  19.5 us (2%)
    ppermute x4, waiting for transfers between devices, gather_around(): from_left = lax.ppermute(from_left, axis, ahead)  74.5 us
    reduce_scatter x1, waiting for transfers between devices, per_device(): lax.psum_scatter(jnp.dot(attended, w_out, preferred_element_type=jnp.floa...  71.6 us
    reduce_scatter x1, waiting for transfers between devices, per_device(): lax.psum_scatter(grad_qkv.reshape(D, 3, width_local).astype(jnp.bfloat16)...  67 us
    dynamic_update_slice x8, local copies, waits for them, and re-layouts, backward_row(): lax.scan(backward_block, (zeros_acc, zeros_acc), block_inputs)  46.6 us
    dot_general x4, matrix products, backward_block(): jnp.einsum('qhd,khd->hqk', grad_block, value_row, preferred_element_type=...  46.2 us
    reduce_scatter x1, waiting for transfers between devices, per_device(): lax.psum_scatter(jnp.dot(hidden, w_down, preferred_element_type=jnp.float...  44.4 us
    convert_element_type x4, other arithmetic, backward_block(): score_grad = (probs_block * (prob_grad - row_inner)).astype(jnp.bfloat16)  44.2 us
    dot_general x4, matrix products, contract_cols(): lax.dot_general(left, right, (((1,), (1,)), ((), ())), preferred_element_...  43.8 us
  transfers between devices with their start and end apart: 21, of which 13 were waited for; matrix products, arithmetic and copies ran while one was open for 35% of the time, Pallas kernels for 0%

profile of v1, /device:TPU:0, one launch (start us, length us, event | category | flops | bytes accessed | tf_op | source)
XLA Modules:
  0.0 1055.0 jit_solution(15009828789300184077)
XLA Ops:
  16.8 36.3 %all_gather.23 = bf16[256,1024]{1,0:T(8,128)(2,1)} all-gather(bf16[32,1024]{1,0:T(8,128)(2,1)S(1)} %convert_element_type.159), channel_id=1, replica_groups=mesh['dp'=8,'tensor'=4] {'dp'}, dimensions={0}, use_global_device_ids=true | all-gather | bytes 589824 | tf_op jit(solution)/shard_map/all_gather | solution.py:141
  54.1 7.5 all-gather.9.cloned.1.call-done
  61.6 35.9 %all-gather.7.cloned.1.call-done = bf16[2048,1024]{1,0:T(8,128)(2,1)} async-done(((bf16[512,1024]{1,0:T(8,128)(2,1)}), bf16[2048,1024]{1,0:T(8,128)(2,1)}) %all-gather.7.cloned.1.call-update) | async-done | bytes 4194320 | tf_op jit(solution)/shard_map/all_gather | solution.py:153
  97.5 6.2 fusion.48
  110.1 57.2 %while.47 = (s32[]{:T(128)}, bf16[4,512,4,64]{1,3,2,0:T(8,128)(2,1)}, f32[4,4,512,1]{2,1,3,0:T(4,128)}, s32[4,512]{1,0:T(4,128)S(1)}, s32[2048]{0:T(1024)S(1)}, ...) while((s32[]{:T(128)}, ...), condition=%wide.region_8.9_spmd, body=%wide.region_5.8_spmd.sunk | while | flops 1121056768 | bytes 57227380 | solution.py:184
  176.2 71.6 %reduce-scatter.8.cloned.1.call-done = f32[512,1024]{1,0:T(8,128)} async-done(((f32[2048,1024]{1,0:T(8,128)}), f32[512,1024]{1,0:T(8,128)}) %reduce-scatter.8.cloned.1.call-update) | async-done | bytes 2097168 | tf_op jit(solution)/shard_map/reduce_scatter | solution.py:194
  264.4 19.2 %collective-permute-done = bf16[128,2,1024]{2,1,0:T(2,128)(2,1)S(1)} collective-permute-done((bf16[128,2,1024]{2,1,0:T(2,128)(2,1)S(1)}, bf16[128,2,1024]{2,1,0:T(2,128)(2,1)S(1)}, u32[]{:S(2)}, u32[]{:S(2)}) %collective-permute-start) | collective-permute-done | bytes 524320 | tf_op jit(solution)/shard_map/ppermute | solution.py:33
  289.6 20.9 %collective-permute-done.2 = bf16[128,2,1024]{2,1,0:T(2,128)(2,1)} collective-permute-done((bf16[128,2,1024]{2,1,0:T(2,128)(2,1)S(1)}, bf16[128,2,1024]{2,1,0:T(2,128)(2,1)}, u32[]{:S(2)}, u32[]{:S(2)}) %collective-permute-start.2) | collective-permute-done | bytes 524320 | tf_op jit(solution)/shard_map/ppermute | solution.py:33
  318.1 27.8 %collective-permute-done.4 = bf16[128,2,1024]{2,1,0:T(2,128)(2,1)} collective-permute-done((bf16[128,2,1024]{2,1,0:T(2,128)(2,1)}, bf16[128,2,1024]{2,1,0:T(2,128)(2,1)}, u32[]{:S(2)}, u32[]{:S(2)}) %collective-permute-start.4) | collective-permute-done | bytes 524320 | tf_op jit(solution)/shard_map/ppermute | solution.py:33
  358.3 6.6 collective-permute-done.6
  366.1 6.0 copy.103
  372.1 15.5 %fusion.96 = f32[2048,2048]{1,0:T(8,128)} fusion(bf16[2048,1024]{1,0:T(8,128)(2,1)} %all-gather.11.cloned.1.call-done, bf16[1024,2048]{1,0:T(8,128)(2,1)} %bitcast.175), kind=kOutput, calls=%fused_computation.188 | convolution fusion | flops 8589934592 | bytes 25165824 | tf_op jit(solution)/shard_map/dot_general | solution.py:202
  387.6 8.3 all-gather.15.cloned.1.call-done
  395.9 17.2 %fusion.73 = (f32[2048,1024]{1,0:T(8,128)}, f32[2048,1024]{1,0:T(8,128)}, bf16[2048,1024]{1,0:T(8,128)(2,1)}) fusion(f32[2048,2048]{1,0:T(8,128)} %fusion.96, bf16[2048,1024]{1,0:T(8,128)(2,1)} %all-gather.15.cloned.1.call-done, bf16[1024,1024]{1,0:T(8,128)(2,1)} %all-gather.13.cloned.1.call-done), kind=kOutput, calls=%fused_computation.124 | convolution fusion | flops 4324327424 | bytes 44040192 | tf_op jit(solution)/shard_map/dot_general | solution.py:106
  413.1 15.1 %convolution_convert_fusion.1 = bf16[2048,1024]{1,0:T(8,128)(2,1)} fusion(bf16[1024,2048]{1,0:T(8,128)(2,1)} %bitcast.176, f32[2048,1024]{1,0:T(8,128)} %get-tuple-element.340, f32[2048,1024]{1,0:T(8,128)} %get-tuple-element.339), kind=kOutput, calls=%fused_computation.65 | convolution fusion | flops 8600420352 | bytes 25165824 | tf_op jit(solution)/shard_map/dot_general | solution.py:106
  428.5 9.6 convolution_convert_fusion.3
  438.2 34.7 %reduce-scatter.12.cloned.1.call-done = bf16[512,1024]{1,0:T(8,128)(2,1)} async-done(((bf16[2048,1024]{1,0:T(8,128)(2,1)}), bf16[512,1024]{1,0:T(8,128)(2,1)}) %reduce-scatter.12.cloned.1.call-update) | async-done | bytes 1048592 | tf_op jit(solution)/shard_map/reduce_scatter | solution.py:217
  475.6 44.4 %reduce-scatter.10.cloned.1.call-done = bf16[512,1024]{1,0:T(8,128)(2,1)} async-done(((bf16[2048,1024]{1,0:T(8,128)(2,1)}), bf16[512,1024]{1,0:T(8,128)(2,1)}) %reduce-scatter.10.cloned.1.call-update) | async-done | bytes 1048592 | tf_op jit(solution)/shard_map/reduce_scatter | solution.py:204
  526.1 17.1 %convolution_convert_fusion = bf16[1024,2048]{1,0:T(8,128)(2,1)} fusion(bf16[2048,1024]{1,0:T(8,128)(2,1)} %all-gather.11.cloned.1.call-done, f32[2048,1024]{1,0:T(8,128)} %get-tuple-element.340, f32[2048,1024]{1,0:T(8,128)} %get-tuple-element.339), kind=kOutput, calls=%fused_computation.64 | convolution fusion | flops 8600420352 | bytes 25165824 | tf_op jit(solution)/shard_map/dot_general | solution.py:100
  543.1 7.8 convert_element_type.182
  551.1 9.5 convolution_convert_fusion.5
  570.8 230.6 %while.48 = (s32[]{:T(128)}, f32[2048,4,64]{0,2,1:T(8,128)}, f32[2048,4,64]{0,2,1:T(8,128)}, f32[4,512,4,64]{1,0,3,2:T(4,128)}, bf16[4,512,4,64]{1,3,2,0:T(8,128...) while((s32[]{:T(128)}, f32[2048,4,64]{0,2,1:T(8,128)}, ...), condition=%wide.region_18.19_spmd.clone, body=%wide.region_16.18_spmd.clone.sunk | while | flops 2751068160 | bytes 183179600 | solution.py:267
  576.1 7.2 fusion.156
  583.4 11.5 %multiply_reduce_fusion.4 = (f32[4,512]{1,0:T(4,128)}, f32[4,512,2048]{2,1,0:T(8,128)}) fusion(f32[4,512,2048]{2,1,0:T(8,128)S(1)} %fusion.154, f32[4,512]{1,0:T(4,128)S(1)} %dynamic-slice_bitcast_fusion.2, pred[512,2048]{1,0:T(8,128)(4,1)} %copy-done.1, bf16[2048,4,64]{0,2,1:T(8,128)(2,1)} %get-tuple-element.554, ...), kind=kOutput, calls=%fused_computation.20.clone.1 | convolution fusion | flops 557840384 | bytes 35930116 | tf_op jit(solution)/shard_map/while/body/eval_jaxpr/while/body/eval_jaxpr/qhd,khd->hqk/dot_general | solution.py:239
  594.9 11.1 %multiply_convert_fusion.4 = bf16[4,512,2048]{2,1,0:T(8,128)(2,1)} fusion(f32[4,512,2048]{2,1,0:T(8,128)} %get-tuple-element.489, f32[4,512,2048]{2,1,0:T(8,128)S(1)} %fusion.154, f32[4,512]{1,0:T(4,128)} %get-tuple-element.490, f32[4,512]{1,0:T(4,128)S(1)} %dynamic-slice_bitcast_fusion.2, pred[512,2048]{1,0:T(8,128)(4,1)} %copy-done.1), kind=kLoop, calls=%fused_computation.19.clone.1 | loop fusion | flops 25165824 | bytes 43008000 | tf_op jit(solution)/shard_map/while/body/eval_jaxpr/while/body/eval_jaxpr/convert_element_type | solution.py:243
  606.0 6.2 fusion.157
  616.8 11.1 %dynamic_update_slice.73 = f32[4,512,4,64]{1,0,3,2:T(4,128)} dynamic-update-slice(f32[4,512,4,64]{1,0,3,2:T(4,128)} %get-tuple-element.534, f32[1,512,4,64]{1,0,3,2:T(1,128)S(1)} %copy.107, s32[]{:T(128)S(6)} %copy.133, s32[]{:T(128)} %constant.205.clone.1..sunk, s32[]{:T(128)} %constant.205.clone.1..sunk, s32[]{:T(128)} %constant.205.clone.1..sunk) | dynamic-update-slice | bytes 1048580 | tf_op jit(solution)/shard_map/while/body/eval_jaxpr/while/body/jit(dynamic_update_index_in_dim)/dynamic_update_slice | solution.py:267
  632.8 7.6 fusion.156
  640.5 11.6 %multiply_reduce_fusion.4 = (f32[4,512]{1,0:T(4,128)}, f32[4,512,2048]{2,1,0:T(8,128)}) fusion(f32[4,512,2048]{2,1,0:T(8,128)S(1)} %fusion.154, f32[4,512]{1,0:T(4,128)S(1)} %dynamic-slice_bitcast_fusion.2, pred[512,2048]{1,0:T(8,128)(4,1)} %copy-done.1, bf16[2048,4,64]{0,2,1:T(8,128)(2,1)} %get-tuple-element.554, ...), kind=kOutput, calls=%fused_computation.20.clone.1 | convolution fusion | flops 557840384 | bytes 35930116 | tf_op jit(solution)/shard_map/while/body/eval_jaxpr/while/body/eval_jaxpr/qhd,khd->hqk/dot_general | solution.py:239
  652.0 11.1 %multiply_convert_fusion.4 = bf16[4,512,2048]{2,1,0:T(8,128)(2,1)} fusion(f32[4,512,2048]{2,1,0:T(8,128)} %get-tuple-element.489, f32[4,512,2048]{2,1,0:T(8,128)S(1)} %fusion.154, f32[4,512]{1,0:T(4,128)} %get-tuple-element.490, f32[4,512]{1,0:T(4,128)S(1)} %dynamic-slice_bitcast_fusion.2, pred[512,2048]{1,0:T(8,128)(4,1)} %copy-done.1), kind=kLoop, calls=%fused_computation.19.clone.1 | loop fusion | flops 25165824 | bytes 43008000 | tf_op jit(solution)/shard_map/while/body/eval_jaxpr/while/body/eval_jaxpr/convert_element_type | solution.py:243
  663.1 6.2 fusion.157
  674.7 11.1 %dynamic_update_slice.73 = f32[4,512,4,64]{1,0,3,2:T(4,128)} dynamic-update-slice(f32[4,512,4,64]{1,0,3,2:T(4,128)} %get-tuple-element.534, f32[1,512,4,64]{1,0,3,2:T(1,128)S(1)} %copy.107, s32[]{:T(128)S(6)} %copy.133, s32[]{:T(128)} %constant.205.clone.1..sunk, s32[]{:T(128)} %constant.205.clone.1..sunk, s32[]{:T(128)} %constant.205.clone.1..sunk) | dynamic-update-slice | bytes 1048580 | tf_op jit(solution)/shard_map/while/body/eval_jaxpr/while/body/jit(dynamic_update_index_in_dim)/dynamic_update_slice | solution.py:267
  690.8 7.6 fusion.156
  698.4 11.6 %multiply_reduce_fusion.4 = (f32[4,512]{1,0:T(4,128)}, f32[4,512,2048]{2,1,0:T(8,128)}) fusion(f32[4,512,2048]{2,1,0:T(8,128)S(1)} %fusion.154, f32[4,512]{1,0:T(4,128)S(1)} %dynamic-slice_bitcast_fusion.2, pred[512,2048]{1,0:T(8,128)(4,1)} %copy-done.1, bf16[2048,4,64]{0,2,1:T(8,128)(2,1)} %get-tuple-element.554, ...), kind=kOutput, calls=%fused_computation.20.clone.1 | convolution fusion | flops 557840384 | bytes 35930116 | tf_op jit(solution)/shard_map/while/body/eval_jaxpr/while/body/eval_jaxpr/qhd,khd->hqk/dot_general | solution.py:239
  710.0 11.0 %multiply_convert_fusion.4 = bf16[4,512,2048]{2,1,0:T(8,128)(2,1)} fusion(f32[4,512,2048]{2,1,0:T(8,128)} %get-tuple-element.489, f32[4,512,2048]{2,1,0:T(8,128)S(1)} %fusion.154, f32[4,512]{1,0:T(4,128)} %get-tuple-element.490, f32[4,512]{1,0:T(4,128)S(1)} %dynamic-slice_bitcast_fusion.2, pred[512,2048]{1,0:T(8,128)(4,1)} %copy-done.1), kind=kLoop, calls=%fused_computation.19.clone.1 | loop fusion | flops 25165824 | bytes 43008000 | tf_op jit(solution)/shard_map/while/body/eval_jaxpr/while/body/eval_jaxpr/convert_element_type | solution.py:243
  721.0 6.2 fusion.157
  732.4 11.1 %dynamic_update_slice.73 = f32[4,512,4,64]{1,0,3,2:T(4,128)} dynamic-update-slice(f32[4,512,4,64]{1,0,3,2:T(4,128)} %get-tuple-element.534, f32[1,512,4,64]{1,0,3,2:T(1,128)S(1)} %copy.107, s32[]{:T(128)S(6)} %copy.133, s32[]{:T(128)} %constant.205.clone.1..sunk, s32[]{:T(128)} %constant.205.clone.1..sunk, s32[]{:T(128)} %constant.205.clone.1..sunk) | dynamic-update-slice | bytes 1048580 | tf_op jit(solution)/shard_map/while/body/eval_jaxpr/while/body/jit(dynamic_update_index_in_dim)/dynamic_update_slice | solution.py:267
  748.5 7.6 fusion.156
  756.1 11.6 %multiply_reduce_fusion.4 = (f32[4,512]{1,0:T(4,128)}, f32[4,512,2048]{2,1,0:T(8,128)}) fusion(f32[4,512,2048]{2,1,0:T(8,128)S(1)} %fusion.154, f32[4,512]{1,0:T(4,128)S(1)} %dynamic-slice_bitcast_fusion.2, pred[512,2048]{1,0:T(8,128)(4,1)} %copy-done.1, bf16[2048,4,64]{0,2,1:T(8,128)(2,1)} %get-tuple-element.554, ...), kind=kOutput, calls=%fused_computation.20.clone.1 | convolution fusion | flops 557840384 | bytes 35930116 | tf_op jit(solution)/shard_map/while/body/eval_jaxpr/while/body/eval_jaxpr/qhd,khd->hqk/dot_general | solution.py:239
  767.7 11.0 %multiply_convert_fusion.4 = bf16[4,512,2048]{2,1,0:T(8,128)(2,1)} fusion(f32[4,512,2048]{2,1,0:T(8,128)} %get-tuple-element.489, f32[4,512,2048]{2,1,0:T(8,128)S(1)} %fusion.154, f32[4,512]{1,0:T(4,128)} %get-tuple-element.490, f32[4,512]{1,0:T(4,128)S(1)} %dynamic-slice_bitcast_fusion.2, pred[512,2048]{1,0:T(8,128)(4,1)} %copy-done.1), kind=kLoop, calls=%fused_computation.19.clone.1 | loop fusion | flops 25165824 | bytes 43008000 | tf_op jit(solution)/shard_map/while/body/eval_jaxpr/while/body/eval_jaxpr/convert_element_type | solution.py:243
  778.7 6.2 fusion.157
  790.2 11.1 %dynamic_update_slice.73 = f32[4,512,4,64]{1,0,3,2:T(4,128)} dynamic-update-slice(f32[4,512,4,64]{1,0,3,2:T(4,128)} %get-tuple-element.534, f32[1,512,4,64]{1,0,3,2:T(1,128)S(1)} %copy.107, s32[]{:T(128)S(6)} %copy.133, s32[]{:T(128)} %constant.205.clone.1..sunk, s32[]{:T(128)} %constant.205.clone.1..sunk, s32[]{:T(128)} %constant.205.clone.1..sunk) | dynamic-update-slice | bytes 1048580 | tf_op jit(solution)/shard_map/while/body/eval_jaxpr/while/body/jit(dynamic_update_index_in_dim)/dynamic_update_slice | solution.py:267
  821.0 7.0 convolution_convert_fusion.2
  834.4 37.3 %reduce-scatter.18.cloned.1.call-done = bf16[32,1024]{1,0:T(8,128)(2,1)} async-done(((bf16[256,1024]{1,0:T(8,128)(2,1)}), bf16[32,1024]{1,0:T(8,128)(2,1)}) %reduce-scatter.18.cloned.1.call-update) | async-done | bytes 65552 | tf_op jit(solution)/shard_map/reduce_scatter | solution.py:299
  873.2 67.0 %reduce-scatter.16.cloned.1.call-done = bf16[128,3,256]{2,0,1:T(8,128)(2,1)} async-done(((bf16[1024,3,256]{2,0,1:T(8,128)(2,1)}), bf16[128,3,256]{2,0,1:T(8,128)(2,1)}) %reduce-scatter.16.cloned.1.call-update) | async-done | bytes 196624 | tf_op jit(solution)/shard_map/reduce_scatter | solution.py:293
  944.4 41.8 %reduce-scatter.14.cloned.1.call-done = bf16[512,1024]{1,0:T(8,128)(2,1)} async-done(((bf16[2048,1024]{1,0:T(8,128)(2,1)}), bf16[512,1024]{1,0:T(8,128)(2,1)}) %reduce-scatter.14.cloned.1.call-update) | async-done | bytes 1048592 | tf_op jit(solution)/shard_map/reduce_scatter | solution.py:284
  990.4 39.7 %all-reduce.7 = (f32[]{:T(128)}, f32[2,1024]{1,0:T(2,128)S(1)}) all-reduce(f32[]{:T(128)S(6)} %add.287, f32[2,1024]{1,0:T(2,128)S(1)} %pad_maximum_fusion.1), channel_id=1, replica_groups=mesh['dp'=8,'tensor'=4] {'dp','tensor'}, use_global_device_ids=true, to_apply=%region_30.31 | all-reduce | flops 2049 | bytes 16392 | tf_op jit(solution)/shard_map/psum | solution.py:319
  1037.1 6.5 multiply_subtract_fusion
  (318 shorter events, 226.8 us)
Async XLA Ops:
  7.2 9.1 copy-start.53
  7.2 9.6 copy-start.29
  7.2 54.4 %all-gather.9.cloned.1.call-start = ((), (), s32[]{:S(2)}) async-start(), calls=%async_computation.8 | async-start | bytes 1769472 | tf_op jit(solution)/shard_map/all_gather | solution.py:140
  9.1 88.4 %all-gather.7.cloned.1.call-start = ((), (), s32[]{:S(2)}) async-start(), calls=%async_computation.7 | async-start | bytes 5242880 | tf_op jit(solution)/shard_map/all_gather | solution.py:153
  16.3 231.6 %reduce-scatter.8.cloned.1.call-start = ((), (), s32[]{:S(2)}) async-start(), calls=%async_computation.9 | async-start | bytes 10485760 | tf_op jit(solution)/shard_map/reduce_scatter | solution.py:194
  54.1 50.3 %copy-start.14 = (f32[2048,32]{0,1:T(8,128)}, f32[2048,32]{0,1:T(8,128)S(1)}, u32[]{:S(2)}) copy-start(f32[2048,32]{0,1:T(8,128)S(1)} %get-tuple-element.357) | copy-start | bytes 786436
  54.1 50.3 %copy-start.16 = (f32[2048,32]{0,1:T(8,128)}, f32[2048,32]{0,1:T(8,128)S(1)}, u32[]{:S(2)}) copy-start(f32[2048,32]{0,1:T(8,128)S(1)} %get-tuple-element.358) | copy-start | bytes 786436
  167.3 8.6 copy-start.4
  167.3 8.6 copy-start.5
  176.0 196.1 %all-gather.11.cloned.1.call-start = ((), (), s32[]{:S(2)}) async-start(), calls=%async_computation.10 | async-start | bytes 5242880 | tf_op jit(solution)/shard_map/all_gather | solution.py:201
  251.7 135.9 %all-gather.13.cloned.1.call-start = ((), (), s32[]{:S(2)}) async-start(), calls=%async_computation.11 | async-start | bytes 2359296 | tf_op jit(solution)/shard_map/all_gather | solution.py:143
  253.6 142.3 %all-gather.15.cloned.1.call-start = ((), (), s32[]{:S(2)}) async-start(), calls=%async_computation.13 | async-start | bytes 5242880 | tf_op jit(solution)/shard_map/all_gather | solution.py:212
  254.2 218.8 %reduce-scatter.12.cloned.1.call-start = ((), (), s32[]{:S(2)}) async-start(), calls=%async_computation.14 | async-start | bytes 5242880 | tf_op jit(solution)/shard_map/reduce_scatter | solution.py:217
  259.7 23.9 %collective-permute-start = (bf16[128,2,1024]{2,1,0:T(2,128)(2,1)S(1)}, bf16[128,2,1024]{2,1,0:T(2,128)(2,1)S(1)}, u32[]{:S(2)}, u32[]{:S(2)}) collective-permute-start(bf16[128,2,1024]{2,1,0:T(2,128)(2,1)S(1)} %get-tuple-element.332), channel_id=1, source_target_pairs={{0,4},{4,8},{8,12},{12,16},{16,20},{20,24},{24,28},{28,0},{1,5},{5... | collective-permute-start | bytes 1572872 | tf_op jit(solution)/shard_map/ppermute | solution.py:33
  261.2 24.9 %collective-permute-start.1 = (bf16[128,2,1024]{2,1,0:T(2,128)(2,1)S(1)}, bf16[128,2,1024]{2,1,0:T(2,128)(2,1)}, u32[]{:S(2)}, u32[]{:S(2)}) collective-permute-start(bf16[128,2,1024]{2,1,0:T(2,128)(2,1)S(1)} %get-tuple-element.332), channel_id=1, source_target_pairs={{0,28},{4,0},{8,4},{12,8},{16,12},{20,16},{24,20},{28,24},{1,29},{... | collective-permute-start | bytes 1572872 | tf_op jit(solution)/shard_map/ppermute | solution.py:38
  283.6 26.9 %collective-permute-start.2 = (bf16[128,2,1024]{2,1,0:T(2,128)(2,1)S(1)}, bf16[128,2,1024]{2,1,0:T(2,128)(2,1)}, u32[]{:S(2)}, u32[]{:S(2)}) collective-permute-start(bf16[128,2,1024]{2,1,0:T(2,128)(2,1)S(1)} %collective-permute-done), channel_id=1, source_target_pairs={{0,4},{4,8},{8,12},{12,16},{16,20},{20,24},{24,28},{28,0},{1,5},{5... | collective-permute-start | bytes 1572872 | tf_op jit(solution)/shard_map/ppermute | solution.py:33
  286.1 27.0 %collective-permute-start.3 = (bf16[128,2,1024]{2,1,0:T(2,128)(2,1)}, bf16[128,2,1024]{2,1,0:T(2,128)(2,1)}, u32[]{:S(2)}, u32[]{:S(2)}) collective-permute-start(bf16[128,2,1024]{2,1,0:T(2,128)(2,1)} %collective-permute-done.1), channel_id=1, source_target_pairs={{0,28},{4,0},{8,4},{12,8},{16,12},{20,16},{24,20},{28,24},{1,29},{... | collective-permute-start | bytes 1572872 | tf_op jit(solution)/shard_map/ppermute | solution.py:38
  310.5 35.4 %collective-permute-start.4 = (bf16[128,2,1024]{2,1,0:T(2,128)(2,1)}, bf16[128,2,1024]{2,1,0:T(2,128)(2,1)}, u32[]{:S(2)}, u32[]{:S(2)}) collective-permute-start(bf16[128,2,1024]{2,1,0:T(2,128)(2,1)} %collective-permute-done.2), channel_id=1, source_target_pairs={{0,4},{4,8},{8,12},{12,16},{16,20},{20,24},{24,28},{28,0},{1,5},{5... | collective-permute-start | bytes 1572872 | tf_op jit(solution)/shard_map/ppermute | solution.py:33
  313.1 44.1 %collective-permute-start.5 = (bf16[128,2,1024]{2,1,0:T(2,128)(2,1)}, bf16[128,2,1024]{2,1,0:T(2,128)(2,1)S(1)}, u32[]{:S(2)}, u32[]{:S(2)}) collective-permute-start(bf16[128,2,1024]{2,1,0:T(2,128)(2,1)} %collective-permute-done.3), channel_id=1, source_target_pairs={{0,28},{4,0},{8,4},{12,8},{16,12},{20,16},{24,20},{28,24},{1,29},{... | collective-permute-start | bytes 1572872 | tf_op jit(solution)/shard_map/ppermute | solution.py:38
  345.9 19.1 %collective-permute-start.6 = (bf16[128,2,1024]{2,1,0:T(2,128)(2,1)}, bf16[128,2,1024]{2,1,0:T(2,128)(2,1)S(1)}, u32[]{:S(2)}, u32[]{:S(2)}) collective-permute-start(bf16[128,2,1024]{2,1,0:T(2,128)(2,1)} %collective-permute-done.4), channel_id=1, source_target_pairs={{0,4},{4,8},{8,12},{12,16},{16,20},{20,24},{24,28},{28,0},{1,5},{5... | collective-permute-start | bytes 1572872 | tf_op jit(solution)/shard_map/ppermute | solution.py:33
  428.2 91.7 %reduce-scatter.10.cloned.1.call-start = ((), (), s32[]{:S(2)}) async-start(), calls=%async_computation.12 | async-start | bytes 5242880 | tf_op jit(solution)/shard_map/reduce_scatter | solution.py:204
  438.1 122.6 %all-gather.17.cloned.1.call-start = ((), (), s32[]{:S(2)}) async-start(), calls=%async_computation.15 | async-start | bytes 5242880 | tf_op jit(solution)/shard_map/all_gather | solution.py:225
  523.4 19.7 %copy-start.46 = (f32[512]{0:T(512)}, f32[512]{0:T(512)S(1)}, u32[]{:S(2)}) copy-start(f32[512]{0:T(512)S(1)} %negate_multiply_fusion.1) | copy-start | bytes 6148
  526.0 303.9 %all-reduce.10.cloned.1.call-start = ((), (), s32[]{:S(2)}) async-start(), calls=%async_computation.20 | async-start | bytes 8388608
  551.0 281.7 %reduce-scatter.20.cloned.1.call-start = ((), (), s32[]{:S(2)}) async-start(), calls=%async_computation.19 | async-start | bytes 2359296 | tf_op jit(solution)/shard_map/reduce_scatter | solution.py:308
  551.1 9.6 copy-start.19
  560.6 311.1 %reduce-scatter.18.cloned.1.call-start = ((), (), s32[]{:S(2)}) async-start(), calls=%async_computation.18 | async-start | bytes 589824 | tf_op jit(solution)/shard_map/reduce_scatter | solution.py:299
  612.3 15.6 %copy-start.22 = (s32[2048]{0:T(1024)S(1)}, s32[2048]{0:T(1024)}, u32[]{:S(2)}) copy-start(s32[2048]{0:T(1024)} %copy-done.21) | copy-start | bytes 24580 | tf_op jit(solution)/shard_map/while/body/eval_jaxpr/while
  612.3 15.6 %copy-start.40 = (s32[4,512]{1,0:T(4,128)S(1)}, s32[4,512]{1,0:T(4,128)}, u32[]{:S(2)}) copy-start(s32[4,512]{1,0:T(4,128)} %copy-done.39) | copy-start | bytes 24580 | tf_op jit(solution)/shard_map/while/body/eval_jaxpr/while
  669.3 16.5 %copy-start.22 = (s32[2048]{0:T(1024)S(1)}, s32[2048]{0:T(1024)}, u32[]{:S(2)}) copy-start(s32[2048]{0:T(1024)} %copy-done.21) | copy-start | bytes 24580 | tf_op jit(solution)/shard_map/while/body/eval_jaxpr/while
  669.3 16.5 %copy-start.40 = (s32[4,512]{1,0:T(4,128)S(1)}, s32[4,512]{1,0:T(4,128)}, u32[]{:S(2)}) copy-start(s32[4,512]{1,0:T(4,128)} %copy-done.39) | copy-start | bytes 24580 | tf_op jit(solution)/shard_map/while/body/eval_jaxpr/while
  727.2 16.3 %copy-start.22 = (s32[2048]{0:T(1024)S(1)}, s32[2048]{0:T(1024)}, u32[]{:S(2)}) copy-start(s32[2048]{0:T(1024)} %copy-done.21) | copy-start | bytes 24580 | tf_op jit(solution)/shard_map/while/body/eval_jaxpr/while
  727.2 16.3 %copy-start.40 = (s32[4,512]{1,0:T(4,128)S(1)}, s32[4,512]{1,0:T(4,128)}, u32[]{:S(2)}) copy-start(s32[4,512]{1,0:T(4,128)} %copy-done.39) | copy-start | bytes 24580 | tf_op jit(solution)/shard_map/while/body/eval_jaxpr/while
  784.9 16.3 %copy-start.22 = (s32[2048]{0:T(1024)S(1)}, s32[2048]{0:T(1024)}, u32[]{:S(2)}) copy-start(s32[2048]{0:T(1024)} %copy-done.21) | copy-start | bytes 24580 | tf_op jit(solution)/shard_map/while/body/eval_jaxpr/while
  784.9 16.3 %copy-start.40 = (s32[4,512]{1,0:T(4,128)S(1)}, s32[4,512]{1,0:T(4,128)}, u32[]{:S(2)}) copy-start(s32[4,512]{1,0:T(4,128)} %copy-done.39) | copy-start | bytes 24580 | tf_op jit(solution)/shard_map/while/body/eval_jaxpr/while
  809.6 130.6 %reduce-scatter.16.cloned.1.call-start = ((), (), s32[]{:S(2)}) async-start(), calls=%async_computation.17 | async-start | bytes 1769472 | tf_op jit(solution)/shard_map/reduce_scatter | solution.py:293
  820.9 165.3 %reduce-scatter.14.cloned.1.call-start = ((), (), s32[]{:S(2)}) async-start(), calls=%async_computation.16 | async-start | bytes 5242880 | tf_op jit(solution)/shard_map/reduce_scatter | solution.py:284
  828.0 158.2 %copy-start.3 = (bf16[512,1024]{1,0:T(8,128)(2,1)S(1)}, bf16[512,1024]{1,0:T(8,128)(2,1)}, u32[]{:S(2)}) copy-start(bf16[512,1024]{1,0:T(8,128)(2,1)} %param.22) | copy-start | bytes 3145732
  828.0 158.2 %copy-start.38 = (f32[1,1024]{1,0:T(1,128)S(1)}, f32[1,1024]{1,0:T(1,128)}, u32[]{:S(2)}) copy-start(f32[1,1024]{1,0:T(1,128)} %copy-done.37) | copy-start | bytes 12292
  828.0 158.2 %copy-start.42 = (f32[512]{0:T(512)S(1)}, f32[512]{0:T(512)}, u32[]{:S(2)}) copy-start(f32[512]{0:T(512)} %copy-done.41) | copy-start | bytes 6148
  828.0 159.9 %copy-start.49 = (f32[512]{0:T(512)S(1)}, f32[512]{0:T(512)}, u32[]{:S(2)}) copy-start(f32[512]{0:T(512)} %copy-done.48) | copy-start | bytes 6148
  828.1 159.9 %copy-start.45 = (f32[512]{0:T(512)S(1)}, f32[512]{0:T(512)}, u32[]{:S(2)}) copy-start(f32[512]{0:T(512)} %copy-done.44) | copy-start | bytes 6148
  828.1 162.3 %copy-start.50 = (f32[1024]{0:T(1024)S(1)}, f32[1024]{0:T(1024)}, u32[]{:S(2)}) copy-start(f32[1024]{0:T(1024)} %get-tuple-element.261) | copy-start | bytes 12292
  828.1 204.1 %copy-start.43 = (f32[2,1024]{1,0:T(2,128)S(1)}, f32[2,1024]{1,0:T(2,128)}, u32[]{:S(2)}) copy-start(f32[2,1024]{1,0:T(2,128)} %param.37) | copy-start | bytes 24580
  828.1 204.1 %copy-start.51 = (f32[2,1024]{1,0:T(2,128)S(1)}, f32[2,1024]{1,0:T(2,128)}, u32[]{:S(2)}) copy-start(f32[2,1024]{1,0:T(2,128)} %param.38) | copy-start | bytes 24580
  828.1 204.1 %copy-start.52 = (f32[2,1024]{1,0:T(2,128)S(1)}, f32[2,1024]{1,0:T(2,128)}, u32[]{:S(2)}) copy-start(f32[2,1024]{1,0:T(2,128)} %param.39) | copy-start | bytes 24580
  828.1 204.8 %copy-start.7 = (f32[512,1024]{1,0:T(8,128)S(1)}, f32[512,1024]{1,0:T(8,128)}, u32[]{:S(2)}) copy-start(f32[512,1024]{1,0:T(8,128)} %copy-done.6) | copy-start | bytes 6291460
  828.1 204.8 %copy-start.47 = (f32[512]{0:T(512)S(1)}, f32[512]{0:T(512)}, u32[]{:S(2)}) copy-start(f32[512]{0:T(512)} %copy-done.46) | copy-start | bytes 6148
  (48 other events, 204.6 us)
Sparse Core Ops, SparseCore 0:
  10.7 50.9 all-gather.8
  63.8 33.7 all-gather.6
  176.1 71.7 reduce-scatter.7
  251.8 34.4 all-gather.10
  289.1 71.5 all-gather.12
  362.2 33.6 all-gather.14
  428.4 44.5 reduce-scatter.11
  475.4 44.4 reduce-scatter.9
  526.2 34.4 all-gather.16
  564.7 156.3 all-reduce.9
  725.0 66.6 reduce-scatter.19
  809.7 61.9 reduce-scatter.17
  875.7 64.4 reduce-scatter.15
  942.7 43.4 reduce-scatter.13
